TPU v7x, 32 devices: a whole 2x2x4 slice. The times are simulated.
32 devices in a mesh: ctx: 8 (over z, y), wsh: 4 (over x, core).
Axes of the slice: x: 2, y: 2, z: 4, core: 2. Of those that a mesh axis runs over, the one named last changes fastest.
Arguments:
- tokens: bfloat16 [4, 1024, 2048], P('wsh', 'ctx'), may hold values from -6 to 6
- out_grad: bfloat16 [4, 1024, 2048], P('wsh', 'ctx'), may hold values from -6 to 6
- attn_weight: bfloat16 [4, 2048, 2048], P(None, None, 'wsh'), may hold values from -0.125 to 0.125
- mlp_weight: bfloat16 [3, 2048, 8192], P(None, None, 'wsh'), may hold values from -0.125 to 0.125
- norm_gains: bfloat16 [4, 2048], P(None, 'wsh'), may hold values from 0.25 to 1.75
- adapt_model: bfloat16 [11, 64, 2048], P(None, None, 'wsh'), may hold values from -0.125 to 0.125
- adapt_hidden: bfloat16 [3, 64, 8192], P(None, None, 'wsh'), may hold values from -0.0625 to 0.0625
- lengths: int32 [4], replicated, may hold values from 512 to 1024, as said below
- adapter_pick: int32 [4], replicated, may hold values from 0 to 3
- block_order: int32 [4, 16], P('wsh'), may hold values from 0 to 15, as said below
Outputs:
- layer_out: bfloat16 [4, 1024, 2048], P('wsh', 'ctx')
- input_grad: float32 [4, 1024, 2048], P('wsh', 'ctx')
- adapt_model_grad: float32 [11, 64, 2048], P(None, None, 'wsh')
- adapt_hidden_grad: float32 [3, 64, 8192], P(None, None, 'wsh')
Inputs may be any that keep to these rules, and one draw needn't show every extreme that they name: `lengths`: some sequence has exactly 1024 valid tokens. Each row of block_order is a permutation of the 16 blocks; the two blocks stored on one index of ctx are p and 15 - p for some p, in either order.
All inputs are finite; a program needn't handle non-finite values.
Results may differ from a plain program's by a relative error of at most 0.017.
Values may be sent and summed in bfloat16 or wider, within the bound.
No kernel may reach another device: no remote copies, remote signals or barrier semaphores. Data moves between devices by JAX's collectives and lax.ppermute only.
A program may use at most 512 MiB of HBM per device.

v0:
```python
import math
import jax
import jax.numpy as jnp
from jax import lax
from jax.sharding import PartitionSpec as P

HEADS = 16
HEAD_DIM = 128
RANK = 16
ADAPTERS = 4
NORM_EPS = 1e-06
ADAPTER_SCALE = 4.0
ROPE_BASE = 500000.0
F32 = jnp.float32
BF16 = jnp.bfloat16
CORE_SWAP = ((0, 1), (1, 0), (2, 3), (3, 2))
CHIP_SWAP = ((0, 2), (2, 0), (1, 3), (3, 1))


def dot(left, right, dims):
    return lax.dot_general(left, right, (dims, ((), ())), preferred_element_type=F32)


def mm(left, right):
    return dot(left, right, ((1,), (0,)))


def mm_t(left, right):
    return dot(left, right, ((1,), (1,)))


def tmm(left, right):
    return dot(left, right, ((0,), (0,)))


def swap_core(values):
    return lax.ppermute(values, "wsh", CORE_SWAP)


def swap_chip(values):
    return lax.ppermute(values, "wsh", CHIP_SWAP)


def sum_wsh(values):
    values = values + swap_core(values)
    return values + swap_chip(values)


def gather_wsh(block, axis, me):
    far = swap_chip(block)
    near = swap_core(block)
    far_near = swap_core(far)
    extent = block.shape[axis]
    shape = list(block.shape)
    shape[axis] = 4 * extent
    whole = jnp.zeros(shape, block.dtype)
    for flip, piece in ((0, block), (1, near), (2, far), (3, far_near)):
        start = [0] * block.ndim
        start[axis] = (me ^ flip) * extent
        whole = lax.dynamic_update_slice(whole, piece, start)
    return whole


def scatter_wsh(partial, axis, me):
    extent = partial.shape[axis] // 4

    def piece(flip):
        return lax.dynamic_slice_in_dim(partial, (me ^ flip) * extent, extent, axis)

    far = piece(2).astype(F32) + swap_core(piece(3)).astype(F32)
    far = swap_chip(far.astype(BF16))
    near = piece(0).astype(F32) + swap_core(piece(1)).astype(F32)
    return near + far.astype(F32)


def rotate(values, cosine, sine_part):
    half = HEAD_DIM // 2
    first, second = (values[..., :half], values[..., half:])
    return jnp.concatenate(
        [first * cosine - second * sine_part, second * cosine + first * sine_part], axis=-1
    )


def per_device(
    tokens,
    out_grad,
    attn_weight,
    mlp_weight,
    norm_gains,
    adapt_model,
    adapt_hidden,
    lengths,
    adapter_pick,
    block_order,
):
    own_rows = tokens[0]
    rows, model_dim = own_rows.shape
    block_rows = rows // 2
    ctx_size = lax.axis_size("ctx")
    seqs = lax.axis_size("wsh")
    width = model_dim // seqs
    local_heads = width // HEAD_DIM
    me = lax.axis_index("wsh")
    ctx_index = lax.axis_index("ctx")
    pairs = seqs * local_heads
    members = math.gcd(ctx_size, pairs)
    groups = ctx_size // members
    per_member = pairs // members
    splits = local_heads // per_member
    group_rows = members * rows
    member = ctx_index % members
    group = ctx_index // members
    ctx_groups = [[g * members + i for i in range(members)] for g in range(groups)]
    key_groups = [[g * members + i for g in range(groups)] for i in range(members)]
    score_scale = HEAD_DIM ** (-0.5)
    all_rows = seqs * rows

    def columns(matrix):
        return lax.dynamic_slice_in_dim(matrix, me * width, width, 1)

    orders = gather_wsh(block_order, 0, me)
    positions = (orders[:, :, None] * block_rows + jnp.arange(block_rows)[None, None, :]).reshape(
        seqs, -1
    )
    row_positions = lax.dynamic_slice_in_dim(positions, ctx_index * rows, rows, 1)
    own_positions = lax.dynamic_index_in_dim(row_positions, me, keepdims=False)
    own_length = lax.dynamic_index_in_dim(lengths, me, keepdims=False)
    valid_rows = (own_positions < own_length).astype(F32)[:, None]
    half_dim = HEAD_DIM // 2
    frequency = ROPE_BASE ** (-(jnp.arange(half_dim, dtype=F32) * 2.0) / HEAD_DIM)
    angles = row_positions.reshape(-1).astype(F32)[:, None] * frequency[None, :]
    cosine, sine_part = (jnp.cos(angles)[:, None, :], jnp.sin(angles)[:, None, :])
    picked = (jnp.arange(ADAPTERS * RANK)[None, :] // RANK == adapter_pick[:, None]).astype(F32)
    row_mask = jnp.broadcast_to(picked[:, None, :], (seqs, rows, ADAPTERS * RANK)).reshape(
        all_rows, -1
    )

    def low(product):
        return (product * row_mask).astype(BF16)

    def low_sum(partial):
        narrow = (partial * row_mask).reshape(all_rows, ADAPTERS, RANK).sum(1)
        total = jnp.tile(sum_wsh(narrow), (1, ADAPTERS))
        return (total * row_mask).astype(BF16)

    gains = norm_gains.astype(F32)
    last_gain = gather_wsh(norm_gains[3:4], 1, me).astype(F32)
    hidden = gather_wsh(own_rows, 0, me)
    rows_a = gather_wsh(jnp.concatenate([adapt_model[:6], adapt_model[10:11]], 0), 2, me)
    low_in = [low(mm_t(hidden, rows_a[k])) for k in range(3)]
    proj = [
        mm(hidden, attn_weight[k]) + ADAPTER_SCALE * mm(low_in[k], adapt_model[6 + k])
        for k in range(3)
    ]
    squares = jnp.stack([jnp.sum(proj[0] * proj[0], -1), jnp.sum(proj[1] * proj[1], -1)])
    scales = lax.rsqrt(sum_wsh(squares) / model_dim + NORM_EPS)[:, :, None]

    def heads(values):
        return values.reshape(all_rows, local_heads, HEAD_DIM)

    turned = [
        rotate(heads(proj[k] * scales[k] * gains[k]), cosine, sine_part).astype(BF16)
        for k in range(2)
    ]
    packed = jnp.stack([turned[0], turned[1], heads(proj[2].astype(BF16))])

    def to_heads(values):
        count = values.shape[0]
        shaped = values.reshape(count, seqs, rows, splits, per_member * HEAD_DIM)
        shaped = shaped.transpose(1, 3, 0, 2, 4).reshape(
            members, count, rows, per_member * HEAD_DIM
        )
        moved = lax.all_to_all(shaped, "ctx", 0, 0, tiled=True, axis_index_groups=ctx_groups)
        moved = moved.transpose(1, 0, 2, 3).reshape(count, group_rows, per_member, HEAD_DIM)
        return moved.transpose(0, 2, 1, 3)

    def to_rows(values):
        count = values.shape[0]
        shaped = values.transpose(0, 2, 1, 3).reshape(count, members, rows, per_member * HEAD_DIM)
        moved = lax.all_to_all(
            shaped.transpose(1, 0, 2, 3), "ctx", 0, 0, tiled=True, axis_index_groups=ctx_groups
        )
        moved = moved.reshape(seqs, splits, count, rows, per_member * HEAD_DIM)
        return moved.transpose(2, 0, 3, 1, 4).reshape(count, all_rows, width)

    queries, keys, values = to_heads(packed)
    if groups > 1:
        keys, values = (
            lax.all_gather(part, "ctx", axis=1, tiled=True, axis_index_groups=key_groups)
            for part in (keys, values)
        )
    seq_here = member * per_member // local_heads
    key_positions = lax.dynamic_index_in_dim(positions, seq_here, keepdims=False)
    query_positions = lax.dynamic_slice_in_dim(key_positions, group * group_rows, group_rows)
    length_here = lax.dynamic_index_in_dim(lengths, seq_here, keepdims=False)
    allowed = (key_positions[None, :] <= query_positions[:, None]) & (
        key_positions[None, :] < length_here
    )

    def batched(left, right, lc, rc):
        return lax.dot_general(
            left, right, (((lc,), (rc,)), ((0,), (0,))), preferred_element_type=F32
        )

    scores = jnp.where(allowed[None], batched(queries, keys, 2, 2) * score_scale, -jnp.inf)
    row_max = jnp.max(scores, axis=-1, keepdims=True)
    log_total = row_max + jnp.log(jnp.sum(jnp.exp(scores - row_max), axis=-1, keepdims=True))
    weights = jnp.exp(scores - log_total).astype(BF16)
    attended = batched(weights, values, 2, 1).astype(BF16)
    attended = to_rows(attended[None])[0]
    attended_full = gather_wsh(attended, 1, me)
    low_out = low(mm_t(attended_full, rows_a[3]))
    branch = mm(attended_full, attn_weight[3]) + ADAPTER_SCALE * mm(low_out, adapt_model[9])
    branch_scale = lax.rsqrt(
        sum_wsh(jnp.sum(branch * branch, -1, keepdims=True)) / model_dim + NORM_EPS
    )
    mid = columns(hidden).astype(F32) + branch * branch_scale * gains[2]
    mid_low = mid.astype(BF16)
    mid_full = gather_wsh(mid_low, 1, me)
    low_gate = low(mm_t(mid_full, rows_a[4]))
    low_up = low(mm_t(mid_full, rows_a[5]))
    gate = mm(mid_full, mlp_weight[0]) + ADAPTER_SCALE * mm(low_gate, adapt_hidden[0])
    up = mm(mid_full, mlp_weight[1]) + ADAPTER_SCALE * mm(low_up, adapt_hidden[1])
    sigmoid_gate = jax.nn.sigmoid(gate)
    silu_gate = gate * sigmoid_gate
    product = (silu_gate * up).astype(BF16)
    low_down_part = mm_t(product, adapt_hidden[2])
    down_part = mm_t(product, mlp_weight[2]) + ADAPTER_SCALE * mm(low(low_down_part), rows_a[6])
    down = scatter_wsh(down_part.astype(BF16), 0, me)
    low_down = low_sum(low_down_part)
    down_scale = lax.rsqrt(jnp.mean(down * down, axis=-1, keepdims=True) + NORM_EPS)
    mid_rows = lax.dynamic_slice_in_dim(mid_full, me * rows, rows, 0).astype(F32)
    result = mid_rows + down * down_scale * last_gain
    upstream = out_grad[0].astype(F32) * valid_rows
    scaled = upstream * last_gain
    grad_down = (
        down_scale * scaled - down * down_scale**3 * jnp.mean(scaled * down, axis=-1, keepdims=True)
    ).astype(BF16)
    grad_down = gather_wsh(grad_down, 0, me)
    grad_low_down = low(ADAPTER_SCALE * mm_t(grad_down, rows_a[6]))
    grad_product = mm(grad_down, mlp_weight[2]) + mm(grad_low_down, adapt_hidden[2])
    grad_gate = (grad_product * up * sigmoid_gate * (1.0 + gate * (1.0 - sigmoid_gate))).astype(
        BF16
    )
    grad_up = (grad_product * silu_gate).astype(BF16)
    low_gate_part = ADAPTER_SCALE * mm_t(grad_gate, adapt_hidden[0])
    low_up_part = ADAPTER_SCALE * mm_t(grad_up, adapt_hidden[1])
    own_block = (jnp.arange(seqs) == me).astype(F32)[:, None, None]
    mid_part = (
        mm_t(grad_gate, mlp_weight[0])
        + mm_t(grad_up, mlp_weight[1])
        + mm(low(low_gate_part), rows_a[4])
        + mm(low(low_up_part), rows_a[5])
        + (own_block * upstream[None]).reshape(all_rows, model_dim)
    )
    grad_mid = scatter_wsh(mid_part.astype(BF16), 1, me)
    grad_low_gate = low_sum(low_gate_part)
    grad_low_up = low_sum(low_up_part)
    hidden_grads = jnp.stack(
        [
            ADAPTER_SCALE * tmm(low_gate, grad_gate),
            ADAPTER_SCALE * tmm(low_up, grad_up),
            tmm(grad_low_down, product),
        ]
    )
    grad_a_gate = tmm(grad_low_gate, mid_low)
    grad_a_up = tmm(grad_low_up, mid_low)
    grad_b_down = ADAPTER_SCALE * tmm(low_down, columns(grad_down))
    scaled = grad_mid * gains[2]
    mean = sum_wsh(jnp.sum(scaled * branch, axis=-1, keepdims=True)) / model_dim
    grad_branch = (branch_scale * scaled - branch * branch_scale**3 * mean).astype(BF16)
    low_out_part = ADAPTER_SCALE * mm_t(grad_branch, adapt_model[9])
    attended_part = mm_t(grad_branch, attn_weight[3]) + mm(low(low_out_part), rows_a[3])
    grad_attended = scatter_wsh(attended_part.astype(BF16), 1, me).astype(BF16)
    grad_low_out = low_sum(low_out_part)
    grad_b_out = ADAPTER_SCALE * tmm(low_out, grad_branch)
    grad_a_out = tmm(grad_low_out, attended)
    grad_heads = to_heads(grad_attended[None])[0]
    scores = jnp.where(allowed[None], batched(queries, keys, 2, 2) * score_scale, -jnp.inf)
    weights_full = jnp.exp(scores - log_total)
    grad_probs = batched(grad_heads, values, 2, 2)
    delta = jnp.sum(weights_full * grad_probs, axis=-1, keepdims=True)
    grad_scores = (weights_full * (grad_probs - delta)).astype(BF16)
    grad_queries = batched(grad_scores, keys, 2, 1) * score_scale
    grad_keys = batched(grad_scores, queries, 1, 1) * score_scale
    grad_values = batched(weights_full.astype(BF16), grad_heads, 1, 1)
    if groups > 1:
        grad_keys, grad_values = (
            lax.psum_scatter(
                part, "ctx", scatter_dimension=1, tiled=True, axis_index_groups=key_groups
            )
            for part in (grad_keys, grad_values)
        )
    grads = to_rows(jnp.stack([grad_queries, grad_keys, grad_values]).astype(BF16))
    turned = [
        rotate(heads(grads[k].astype(F32)), cosine, -sine_part).reshape(all_rows, width) * gains[k]
        for k in range(2)
    ]
    sums = jnp.stack([jnp.sum(turned[k] * proj[k], -1) for k in range(2)])
    means = (sum_wsh(sums) / model_dim)[:, :, None]
    grad_proj = [
        (scales[k] * turned[k] - proj[k] * scales[k] ** 3 * means[k]).astype(BF16) for k in range(2)
    ] + [grads[2]]
    low_parts = [ADAPTER_SCALE * mm_t(grad_proj[k], adapt_model[6 + k]) for k in range(3)]
    own_column = (jnp.arange(seqs) == me).astype(F32)[None, :, None]
    input_part = (
        mm_t(grad_proj[0], attn_weight[0])
        + mm_t(grad_proj[1], attn_weight[1])
        + mm_t(grad_proj[2], attn_weight[2])
        + mm(low(low_parts[0]), rows_a[0])
        + mm(low(low_parts[1]), rows_a[1])
        + mm(low(low_parts[2]), rows_a[2])
        + (own_column * grad_mid[:, None, :]).reshape(all_rows, model_dim)
    )
    grad_inputs = scatter_wsh(input_part.astype(BF16), 0, me)
    own_hidden = columns(hidden)
    grad_a_in = [tmm(low_sum(low_parts[k]), own_hidden) for k in range(3)]
    grad_b_in = [ADAPTER_SCALE * tmm(low_in[k], grad_proj[k]) for k in range(3)]
    model_grads = jnp.stack(
        grad_a_in + [grad_a_out, grad_a_gate, grad_a_up] + grad_b_in + [grad_b_out, grad_b_down]
    )
    model_grads = lax.psum(model_grads, "ctx")
    hidden_grads = lax.psum(hidden_grads, "ctx")
    return (result.astype(BF16)[None], grad_inputs[None], model_grads, hidden_grads)


def solution(mesh):
    in_specs = (
        P("wsh", "ctx", None),
        P("wsh", "ctx", None),
        P(None, None, "wsh"),
        P(None, None, "wsh"),
        P(None, "wsh"),
        P(None, None, "wsh"),
        P(None, None, "wsh"),
        P(),
        P(),
        P("wsh", None),
    )
    out_specs = (
        P("wsh", "ctx", None),
        P("wsh", "ctx", None),
        P(None, None, "wsh"),
        P(None, None, "wsh"),
    )
    return jax.shard_map(
        per_device, mesh=mesh, in_specs=in_specs, out_specs=out_specs, check_vma=False
    )
```

profile of v0, /device:TPU:0, one launch (start us, length us, event | category | flops | bytes accessed | tf_op | source)
XLA Modules:
  0.0 655.7 jit_solution(950616927271443762)
XLA Ops:
  20.7 15.3 %collective-permute-done.7 = bf16[7,64,512]{2,1,0:T(8,128)(2,1)} collective-permute-done((bf16[7,64,512]{2,1,0:T(8,128)(2,1)}, bf16[7,64,512]{2,1,0:T(8,128)(2,1)}, u32[]{:S(2)}, u32[]{:S(2)}) %collective-permute-start.7) | collective-permute-done | bytes 458784 | tf_op jit(solution)/shard_map/ppermute | solution.py:41
  72.2 6.4 all-to-all-start
  81.7 34.0 %all-to-all-done = bf16[8,3,128,256]{3,2,1,0:T(8,128)(2,1)} async-done(((bf16[8,3,128,256]{3,2,1,0:T(8,128)(2,1)}), bf16[8,3,128,256]{3,2,1,0:T(8,128)(2,1)}, u32[]{:S(2)}, u32[]{:S(2)}) %all-to-all-start) | async-done | bytes 1572896 | tf_op jit(solution)/shard_map/all_to_all | solution.py:173
  139.1 18.4 %all_to_all.20 = bf16[8,1,128,256]{2,3,1,0:T(8,128)(2,1)} all-to-all(bf16[8,1,128,256]{2,3,1,0:T(8,128)(2,1)S(1)} %copy.165), channel_id=1, replica_groups={{0,4,8,12,16,20,24,28},{1,5,9,13,17,21,25,29},{2,6,10,14,18,22,26,30},{..., dimensions={0} | all-to-all | bytes 1048576 | tf_op jit(solution)/shard_map/all_to_all | solution.py:180
  164.5 11.0 %collective-permute-done.12 = bf16[512,512]{0,1:T(8,128)(2,1)S(1)} collective-permute-done((bf16[512,512]{0,1:T(8,128)(2,1)S(1)}, bf16[512,512]{0,1:T(8,128)(2,1)S(1)}, u32[]{:S(2)}, u32[]{:S(2)}) %collective-permute-start.12) | collective-permute-done | bytes 524320 | tf_op jit(solution)/shard_map/ppermute | solution.py:41
  189.8 11.3 %collective-permute-done.17 = bf16[512,512]{0,1:T(8,128)(2,1)S(1)} collective-permute-done((bf16[512,512]{0,1:T(8,128)(2,1)S(1)}, bf16[512,512]{0,1:T(8,128)(2,1)S(1)}, u32[]{:S(2)}, u32[]{:S(2)}) %collective-permute-start.17) | collective-permute-done | bytes 524320 | tf_op jit(solution)/shard_map/ppermute | solution.py:41
  207.7 11.6 %multiply_add_fusion.1 = f32[512,2048]{0,1:T(8,128)} fusion(f32[512,2048]{0,1:T(8,128)S(1)} %fusion.137, bf16[512,2048]{0,1:T(8,128)(2,1)S(1)} %constant_dynamic-update-slice_fusion.4, bf16[3,2048,2048]{2,1,0:T(8,128)(2,1)} %param.13), kind=kOutput, calls=%fused_computation.37 | convolution fusion | flops 4297064448 | bytes 18874368 | tf_op jit(solution)/shard_map/dot_general | solution.py:21
  219.3 13.1 %multiply_convert_fusion.3 = (bf16[512,2048]{0,1:T(8,128)(2,1)S(1)}, f32[512,2048]{0,1:T(8,128)}) fusion(f32[512,2048]{0,1:T(8,128)} %multiply_add_fusion.1, f32[512,2048]{0,1:T(8,128)S(1)} %fusion.134, bf16[512,2048]{0,1:T(8,128)(2,1)S(1)} %constant_dynamic-update-slice_fusion.4, bf16[3,2048,2048]{2,1,0:T(8,128)(2,1)} %param.13), kind=kOutput, calls=%fused_computation.33 | convolution fusion | flops 4303355904 | bytes 25165824 | tf_op jit(solution)/shard_map/dot_general | solution.py:21
  232.9 7.1 %fusion.2 = f32[512,2048]{0,1:T(8,128)S(1)} fusion(bf16[512,2048]{0,1:T(8,128)(2,1)S(1)} %get-tuple-element.95, bf16[3,2048,2048]{2,1,0:T(8,128)(2,1)} %param.13), kind=kOutput, calls=%fused_computation.2 | convolution fusion | flops 4294967296 | bytes 14680064 | tf_op jit(solution)/shard_map/dot_general | solution.py:21
  250.0 10.0 %collective-permute-done.23 = bf16[1,512]{1,0:T(2,128)(2,1)S(1)} collective-permute-done((bf16[1,512]{1,0:T(2,128)(2,1)S(1)}, bf16[1,512]{1,0:T(2,128)(2,1)S(1)}, u32[]{:S(2)}, u32[]{:S(2)}) %collective-permute-start.23) | collective-permute-done | bytes 1056 | tf_op jit(solution)/shard_map/ppermute | solution.py:41
  268.0 12.4 %collective-permute-done.26 = bf16[128,2048]{0,1:T(8,128)(2,1)S(1)} collective-permute-done((bf16[128,2048]{0,1:T(8,128)(2,1)S(1)}, bf16[128,2048]{0,1:T(8,128)(2,1)S(1)}, u32[]{:S(2)}, u32[]{:S(2)}) %collective-permute-start.26) | collective-permute-done | bytes 524320 | tf_op jit(solution)/shard_map/ppermute | solution.py:41
  284.9 10.0 %multiply_convert_fusion.1 = (bf16[512,2048]{0,1:T(8,128)(2,1)S(1)}, bf16[512,2048]{0,1:T(8,128)(2,1)S(1)}) fusion(f32[512,2048]{0,1:T(8,128)} %multiply_add_fusion.1, f32[512,2048]{0,1:T(8,128)} %get-tuple-element.96, f32[512,2048]{0,1:T(8,128)S(1)} %fusion.130, bf16[512,2048]{0,1:T(8,128)(2,1)S(1)} %constant_dynamic-update-slice_fusion, ...), kind=kOutput, calls=%fused_computation.30 | convolution fusion | flops 4309647360 | bytes 27262976 | tf_op jit(solution)/shard_map/dot_general | solution.py:21
  295.4 7.9 %fusion.8 = f32[512,2048]{0,1:T(8,128)S(1)} fusion(bf16[512,2048]{0,1:T(8,128)(2,1)S(1)} %get-tuple-element.39, bf16[3,2048,2048]{2,1,0:T(8,128)(2,1)} %param.13), kind=kOutput, calls=%fused_computation.8 | convolution fusion | flops 4294967296 | bytes 14680064 | tf_op jit(solution)/shard_map/dot_general | solution.py:21
  303.8 6.9 %fusion.4 = f32[512,2048]{0,1:T(8,128)S(1)} fusion(bf16[512,2048]{0,1:T(8,128)(2,1)S(1)} %get-tuple-element.38, bf16[3,2048,2048]{2,1,0:T(8,128)(2,1)} %param.13), kind=kOutput, calls=%fused_computation.4 | convolution fusion | flops 4294967296 | bytes 14680064 | tf_op jit(solution)/shard_map/dot_general | solution.py:21
  319.4 12.4 %collective-permute-done.30 = bf16[512,512]{0,1:T(8,128)(2,1)S(1)} collective-permute-done((bf16[512,512]{0,1:T(8,128)(2,1)S(1)}, bf16[512,512]{0,1:T(8,128)(2,1)S(1)}, u32[]{:S(2)}, u32[]{:S(2)}) %collective-permute-start.30) | collective-permute-done | bytes 524320 | tf_op jit(solution)/shard_map/ppermute | solution.py:41
  346.0 12.4 %collective-permute-done.35 = bf16[512,512]{1,0:T(8,128)(2,1)S(1)} collective-permute-done((bf16[512,512]{1,0:T(8,128)(2,1)S(1)}, bf16[512,512]{1,0:T(8,128)(2,1)S(1)}, u32[]{:S(2)}, u32[]{:S(2)}) %collective-permute-start.35) | collective-permute-done | bytes 524320 | tf_op jit(solution)/shard_map/ppermute | solution.py:41
  362.5 18.6 %all_to_all.21 = bf16[8,1,128,256]{3,2,1,0:T(8,128)(2,1)} all-to-all(bf16[8,1,128,256]{3,2,1,0:T(8,128)(2,1)S(1)} %bitcast.544), channel_id=1, replica_groups={{0,4,8,12,16,20,24,28},{1,5,9,13,17,21,25,29},{2,6,10,14,18,22,26,30},{..., dimensions={0} | all-to-all | bytes 1048576 | tf_op jit(solution)/shard_map/all_to_all | solution.py:173
  383.1 5.5 fusion.76
  388.6 5.5 multiply_reduce_fusion
  470.0 5.0 fusion.36
  481.6 5.1 fusion.40
  520.6 10.5 %add_convert_fusion = bf16[512,2048]{1,0:T(8,128)(2,1)S(1)} fusion(f32[512,2048]{1,0:T(8,128)} %bitcast.518, f32[512,2048]{1,0:T(8,128)} %fusion.140, f32[512,2048]{1,0:T(8,128)} %fusion.139, f32[512,2048]{1,0:T(8,128)} %fusion.36, f32[512,2048]{1,0:T(8,128)} %fusion.44, f32[512,2048]{1,0:T(8,128)} %fusion.40, f32[2048]{0:T(1024)S(1)} %bitcast.557, ...), kind=kOutput, calls=%fused_computation.28 | convolution fusion | flops 142639104 | bytes 27664384 | tf_op jit(solution)/shard_map/dot_general | solution.py:21
  537.7 10.7 %collective-permute-done.40 = bf16[128,2048]{1,0:T(8,128)(2,1)} collective-permute-done((bf16[128,2048]{1,0:T(8,128)(2,1)S(1)}, bf16[128,2048]{1,0:T(8,128)(2,1)}, u32[]{:S(2)}, u32[]{:S(2)}) %collective-permute-start.40) | collective-permute-done | bytes 524320 | tf_op jit(solution)/shard_map/ppermute | solution.py:41
  551.0 93.8 %all-reduce.3.cloned.1.call-done = (f32[11,64,512]{2,1,0:T(8,128)}, f32[3,64,2048]{2,1,0:T(8,128)}) async-done(((f32[11,64,512]{2,1,0:T(8,128)}, f32[3,64,2048]{2,1,0:T(8,128)}), (f32[11,64,512]{2,1,0:T(8,128)}, f32[3,64,2048]{2,1,0:T(8,128)})) %all-reduce.3.cloned.1.call-update) | async-done | bytes 3014672 | tf_op jit(solution)/shard_map/psum | solution.py:322
  (543 shorter events, 284.6 us)
Async XLA Ops:
  7.2 10.8 %collective-permute-start.4 = (s32[1,16]{1,0:T(1,128)}, s32[1,16]{1,0:T(1,128)S(1)}, u32[]{:S(2)}, u32[]{:S(2)}) collective-permute-start(s32[1,16]{1,0:T(1,128)} %param.19), channel_id=1, source_target_pairs={{0,2},{2,0},{1,3},{3,1},{4,6},{6,4},{5,7},{7,5},{8,10},{10,8},{9,1... | collective-permute-start | bytes 200 | tf_op jit(solution)/shard_map/ppermute | solution.py:41
  11.5 27.8 %collective-permute-start = (bf16[128,2048]{0,1:T(8,128)(2,1)S(1)}, bf16[128,2048]{0,1:T(8,128)(2,1)}, u32[]{:S(2)}, u32[]{:S(2)}) collective-permute-start(bf16[128,2048]{0,1:T(8,128)(2,1)S(1)} %bitcast.539), channel_id=1, source_target_pairs={{0,1},{1,0},{2,3},{3,2},{4,5},{5,4},{6,7},{7,6},{8,9},{9,8},{10,11... | collective-permute-start | bytes 1572872 | tf_op jit(solution)/shard_map/ppermute | solution.py:37
  12.1 26.7 %collective-permute-start.1 = (bf16[128,2048]{0,1:T(8,128)(2,1)S(1)}, bf16[128,2048]{0,1:T(8,128)(2,1)}, u32[]{:S(2)}, u32[]{:S(2)}) collective-permute-start(bf16[128,2048]{0,1:T(8,128)(2,1)S(1)} %bitcast.540), channel_id=1, source_target_pairs={{0,2},{2,0},{1,3},{3,1},{4,6},{6,4},{5,7},{7,5},{8,10},{10,8},{9,1... | collective-permute-start | bytes 1572872 | tf_op jit(solution)/shard_map/ppermute | solution.py:41
  14.7 21.3 %collective-permute-start.6 = (bf16[7,64,512]{2,1,0:T(8,128)(2,1)}, bf16[7,64,512]{2,1,0:T(8,128)(2,1)S(1)}, u32[]{:S(2)}, u32[]{:S(2)}) collective-permute-start(bf16[7,64,512]{2,1,0:T(8,128)(2,1)} %get-tuple-element.59), channel_id=1, source_target_pairs={{0,1},{1,0},{2,3},{3,2},{4,5},{5,4},{6,7},{7,6},{8,9},{9,8},{10,11... | collective-permute-start | bytes 1376264 | tf_op jit(solution)/shard_map/ppermute | solution.py:37
  16.0 20.0 %collective-permute-start.7 = (bf16[7,64,512]{2,1,0:T(8,128)(2,1)}, bf16[7,64,512]{2,1,0:T(8,128)(2,1)}, u32[]{:S(2)}, u32[]{:S(2)}) collective-permute-start(bf16[7,64,512]{2,1,0:T(8,128)(2,1)} %get-tuple-element.59), channel_id=1, source_target_pairs={{0,2},{2,0},{1,3},{3,1},{4,6},{6,4},{5,7},{7,5},{8,10},{10,8},{9,1... | collective-permute-start | bytes 1376264 | tf_op jit(solution)/shard_map/ppermute | solution.py:41
  72.2 43.5 %all-to-all-start = ((bf16[8,3,128,256]{3,2,1,0:T(8,128)(2,1)}), bf16[8,3,128,256]{3,2,1,0:T(8,128)(2,1)}, u32[]{:S(2)}, u32[]{:S(2)}) async-start(bf16[8,3,128,256]{3,2,1,0:T(8,128)(2,1)} %bitcast.528), calls=%async_computation | async-start | bytes 3145728 | tf_op jit(solution)/shard_map/all_to_all | solution.py:173
  162.8 12.7 %collective-permute-start.12 = (bf16[512,512]{0,1:T(8,128)(2,1)S(1)}, bf16[512,512]{0,1:T(8,128)(2,1)S(1)}, u32[]{:S(2)}, u32[]{:S(2)}) collective-permute-start(bf16[512,512]{0,1:T(8,128)(2,1)S(1)} %bitcast.553), channel_id=1, source_target_pairs={{0,2},{2,0},{1,3},{3,1},{4,6},{6,4},{5,7},{7,5},{8,10},{10,8},{9,1... | collective-permute-start | bytes 1572872 | tf_op jit(solution)/shard_map/ppermute | solution.py:41
  164.5 11.3 %collective-permute-start.11 = (bf16[512,512]{0,1:T(8,128)(2,1)S(1)}, bf16[512,512]{0,1:T(8,128)(2,1)S(1)}, u32[]{:S(2)}, u32[]{:S(2)}) collective-permute-start(bf16[512,512]{0,1:T(8,128)(2,1)S(1)} %bitcast.554), channel_id=1, source_target_pairs={{0,1},{1,0},{2,3},{3,2},{4,5},{5,4},{6,7},{7,6},{8,9},{9,8},{10,11... | collective-permute-start | bytes 1572872 | tf_op jit(solution)/shard_map/ppermute | solution.py:37
  188.2 12.8 %collective-permute-start.17 = (bf16[512,512]{0,1:T(8,128)(2,1)S(1)}, bf16[512,512]{0,1:T(8,128)(2,1)S(1)}, u32[]{:S(2)}, u32[]{:S(2)}) collective-permute-start(bf16[512,512]{0,1:T(8,128)(2,1)S(1)} %get-tuple-element.35), channel_id=1, source_target_pairs={{0,2},{2,0},{1,3},{3,1},{4,6},{6,4},{5,7},{7,5},{8,10},{10,8},{9,1... | collective-permute-start | bytes 1572872 | tf_op jit(solution)/shard_map/ppermute | solution.py:41
  189.8 11.3 %collective-permute-start.16 = (bf16[512,512]{0,1:T(8,128)(2,1)S(1)}, bf16[512,512]{0,1:T(8,128)(2,1)S(1)}, u32[]{:S(2)}, u32[]{:S(2)}) collective-permute-start(bf16[512,512]{0,1:T(8,128)(2,1)S(1)} %get-tuple-element.35), channel_id=1, source_target_pairs={{0,1},{1,0},{2,3},{3,2},{4,5},{5,4},{6,7},{7,6},{8,9},{9,8},{10,11... | collective-permute-start | bytes 1572872 | tf_op jit(solution)/shard_map/ppermute | solution.py:37
  242.9 19.3 %collective-permute-start.19 = (bf16[128,2048]{0,1:T(8,128)(2,1)}, bf16[128,2048]{0,1:T(8,128)(2,1)}, u32[]{:S(2)}, u32[]{:S(2)}) collective-permute-start(bf16[128,2048]{0,1:T(8,128)(2,1)} %get-tuple-element.46), channel_id=1, source_target_pairs={{0,1},{1,0},{2,3},{3,2},{4,5},{5,4},{6,7},{7,6},{8,9},{9,8},{10,11... | collective-permute-start | bytes 1572872 | tf_op jit(solution)/shard_map/ppermute | solution.py:37
  245.6 16.6 %collective-permute-start.21 = (bf16[128,2048]{0,1:T(8,128)(2,1)}, bf16[128,2048]{0,1:T(8,128)(2,1)}, u32[]{:S(2)}, u32[]{:S(2)}) collective-permute-start(bf16[128,2048]{0,1:T(8,128)(2,1)} %add_convert_fusion.8), channel_id=1, source_target_pairs={{0,2},{2,0},{1,3},{3,1},{4,6},{6,4},{5,7},{7,5},{8,10},{10,8},{9,1... | collective-permute-start | bytes 1572872 | tf_op jit(solution)/shard_map/ppermute | solution.py:41
  247.2 12.7 %collective-permute-start.23 = (bf16[1,512]{1,0:T(2,128)(2,1)S(1)}, bf16[1,512]{1,0:T(2,128)(2,1)S(1)}, u32[]{:S(2)}, u32[]{:S(2)}) collective-permute-start(bf16[1,512]{1,0:T(2,128)(2,1)S(1)} %get-tuple-element.78), channel_id=1, source_target_pairs={{0,2},{2,0},{1,3},{3,1},{4,6},{6,4},{5,7},{7,5},{8,10},{10,8},{9,1... | collective-permute-start | bytes 3080 | tf_op jit(solution)/shard_map/ppermute | solution.py:41
  247.7 13.6 %collective-permute-start.22 = (bf16[1,512]{1,0:T(2,128)(2,1)S(1)}, bf16[1,512]{1,0:T(2,128)(2,1)S(1)}, u32[]{:S(2)}, u32[]{:S(2)}) collective-permute-start(bf16[1,512]{1,0:T(2,128)(2,1)S(1)} %get-tuple-element.78), channel_id=1, source_target_pairs={{0,1},{1,0},{2,3},{3,2},{4,5},{5,4},{6,7},{7,6},{8,9},{9,8},{10,11... | collective-permute-start | bytes 3080 | tf_op jit(solution)/shard_map/ppermute | solution.py:37
  266.0 14.4 %collective-permute-start.26 = (bf16[128,2048]{0,1:T(8,128)(2,1)S(1)}, bf16[128,2048]{0,1:T(8,128)(2,1)S(1)}, u32[]{:S(2)}, u32[]{:S(2)}) collective-permute-start(bf16[128,2048]{0,1:T(8,128)(2,1)S(1)} %get-tuple-element.33), channel_id=1, source_target_pairs={{0,2},{2,0},{1,3},{3,1},{4,6},{6,4},{5,7},{7,5},{8,10},{10,8},{9,1... | collective-permute-start | bytes 1572872 | tf_op jit(solution)/shard_map/ppermute | solution.py:41
  267.7 12.8 %collective-permute-start.25 = (bf16[128,2048]{0,1:T(8,128)(2,1)S(1)}, bf16[128,2048]{0,1:T(8,128)(2,1)S(1)}, u32[]{:S(2)}, u32[]{:S(2)}) collective-permute-start(bf16[128,2048]{0,1:T(8,128)(2,1)S(1)} %get-tuple-element.33), channel_id=1, source_target_pairs={{0,1},{1,0},{2,3},{3,2},{4,5},{5,4},{6,7},{7,6},{8,9},{9,8},{10,11... | collective-permute-start | bytes 1572872 | tf_op jit(solution)/shard_map/ppermute | solution.py:37
  317.7 14.0 %collective-permute-start.30 = (bf16[512,512]{0,1:T(8,128)(2,1)S(1)}, bf16[512,512]{0,1:T(8,128)(2,1)S(1)}, u32[]{:S(2)}, u32[]{:S(2)}) collective-permute-start(bf16[512,512]{0,1:T(8,128)(2,1)S(1)} %add_convert_fusion.6), channel_id=1, source_target_pairs={{0,2},{2,0},{1,3},{3,1},{4,6},{6,4},{5,7},{7,5},{8,10},{10,8},{9,1... | collective-permute-start | bytes 1572872 | tf_op jit(solution)/shard_map/ppermute | solution.py:41
  344.4 14.0 %collective-permute-start.35 = (bf16[512,512]{1,0:T(8,128)(2,1)S(1)}, bf16[512,512]{1,0:T(8,128)(2,1)S(1)}, u32[]{:S(2)}, u32[]{:S(2)}) collective-permute-start(bf16[512,512]{1,0:T(8,128)(2,1)S(1)} %add_convert_fusion.5), channel_id=1, source_target_pairs={{0,2},{2,0},{1,3},{3,1},{4,6},{6,4},{5,7},{7,5},{8,10},{10,8},{9,1... | collective-permute-start | bytes 1572872 | tf_op jit(solution)/shard_map/ppermute | solution.py:41
  407.2 40.6 %all-to-all-start.3 = ((bf16[8,3,128,256]{2,3,1,0:T(8,128)(2,1)}), bf16[8,3,128,256]{2,3,1,0:T(8,128)(2,1)}, u32[]{:S(2)}, u32[]{:S(2)}) async-start(bf16[8,3,128,256]{2,3,1,0:T(8,128)(2,1)} %copy.187), calls=%async_computation.3 | async-start | bytes 3145728 | tf_op jit(solution)/shard_map/all_to_all | solution.py:180
  411.7 233.1 %all-reduce.3.cloned.1.call-start = ((), (), s32[]{:S(2)}) async-start(), calls=%async_computation.4 | async-start | bytes 6029312 | tf_op jit(solution)/shard_map/psum | solution.py:322
  419.1 10.3 %collective-permute-start.49 = (f32[512,16]{0,1:T(8,128)S(1)}, f32[512,16]{0,1:T(8,128)S(1)}, u32[]{:S(2)}, u32[]{:S(2)}) collective-permute-start(f32[512,16]{0,1:T(8,128)S(1)} %reduce_sum.167), channel_id=1, source_target_pairs={{0,1},{1,0},{2,3},{3,2},{4,5},{5,4},{6,7},{7,6},{8,9},{9,8},{10,11... | collective-permute-start | bytes 98312 | tf_op jit(solution)/shard_map/ppermute | solution.py:37
  430.0 12.5 %collective-permute-start.48 = (f32[512,16]{0,1:T(8,128)S(1)}, f32[512,16]{0,1:T(8,128)S(1)}, u32[]{:S(2)}, u32[]{:S(2)}) collective-permute-start(f32[512,16]{0,1:T(8,128)S(1)} %add.424), channel_id=1, source_target_pairs={{0,2},{2,0},{1,3},{3,1},{4,6},{6,4},{5,7},{7,5},{8,10},{10,8},{9,1... | collective-permute-start | bytes 98312 | tf_op jit(solution)/shard_map/ppermute | solution.py:41
  477.6 22.5 %collective-permute-start.45 = (f32[512,16]{0,1:T(8,128)}, f32[512,16]{0,1:T(8,128)}, u32[]{:S(2)}, u32[]{:S(2)}) collective-permute-start(f32[512,16]{0,1:T(8,128)} %reduce_sum.165), channel_id=1, source_target_pairs={{0,1},{1,0},{2,3},{3,2},{4,5},{5,4},{6,7},{7,6},{8,9},{9,8},{10,11... | collective-permute-start | bytes 98312 | tf_op jit(solution)/shard_map/ppermute | solution.py:37
  534.3 14.1 %collective-permute-start.40 = (bf16[128,2048]{1,0:T(8,128)(2,1)S(1)}, bf16[128,2048]{1,0:T(8,128)(2,1)}, u32[]{:S(2)}, u32[]{:S(2)}) collective-permute-start(bf16[128,2048]{1,0:T(8,128)(2,1)S(1)} %add_convert_fusion.3), channel_id=1, source_target_pairs={{0,2},{2,0},{1,3},{3,1},{4,6},{6,4},{5,7},{7,5},{8,10},{10,8},{9,1... | collective-permute-start | bytes 1572872 | tf_op jit(solution)/shard_map/ppermute | solution.py:41
  (141 other events, 1173.2 us)
Sparse Core Ops, SparseCore 0:
  520.7 124.0 all-reduce.2
where the time goes:
time: 666 us; the launch traced here: 656 us
  waiting for transfers between devices  250 us (38%)
  matrix products  167 us (25%)
  local copies, waits for them, and re-layouts  87.8 us (13%)
  other arithmetic  51.1 us (8%)
  starting transfers between devices  46.8 us (7%)
  blocking collectives  37 us (6%)
  between operations  16.2 us (2%)
    dot_general x56, matrix products, dot(): lax.dot_general(left, right, (dims, ((), ())), preferred_element_type=F32)  145 us
    ppermute x22, waiting for transfers between devices, swap_chip(): return lax.ppermute(values, 'wsh', CHIP_SWAP)  102 us
    psum x1, waiting for transfers between devices, per_device(): model_grads = lax.psum(model_grads, 'ctx')  93.8 us
    all_to_all x1, waiting for transfers between devices, to_heads(): lax.all_to_all(shaped, 'ctx', 0, 0, tiled=True, axis_index_groups=ctx_gro...  34 us
    ppermute x22, starting transfers between devices, swap_chip(): return lax.ppermute(values, 'wsh', CHIP_SWAP)  30 us
    unnamed x222, local copies, waits for them, and re-layouts  22.5 us
    dot_general x6, matrix products, batched(): lax.dot_general(left, right, (((lc,), (rc,)), ((0,), (0,))), preferred_el...  21.8 us
    all_to_all x1, blocking collectives, to_heads(): lax.all_to_all(shaped, 'ctx', 0, 0, tiled=True, axis_index_groups=ctx_gro...  18.6 us
  transfers between devices with their start and end apart: 58, of which 27 were waited for; matrix products, arithmetic and copies ran while one was open for 15% of the time, Pallas kernels for 0%

commit v1 on v0

--- a/solution.py
+++ b/solution.py
@@ -319,7 +319,11 @@
     model_grads = jnp.stack(
         grad_a_in + [grad_a_out, grad_a_gate, grad_a_up] + grad_b_in + [grad_b_out, grad_b_down]
     )
-    model_grads = lax.psum(model_grads, "ctx")
+    model_grads = model_grads
+    for hop in (1, 2, 4):
+        model_grads = model_grads + lax.ppermute(
+            model_grads, "ctx", [(dev, dev ^ hop) for dev in range(8)]
+        )
     hidden_grads = lax.psum(hidden_grads, "ctx")
     return (result.astype(BF16)[None], grad_inputs[None], model_grads, hidden_grads)
 

time: 666 us -> 727 us (1.092)
  waiting for transfers between devices: 250 us -> 324 us
  matrix products: 167 us -> 142 us
  other arithmetic: 51.1 us -> 64.3 us
    ppermute x0 -> x3, waiting for transfers between devices: none -> 113 us  [per_device(): lax.ppermute(model_grads, 'ctx', [(dev, dev ^ hop) for dev in range(8)])]
    psum x1, waiting for transfers between devices: 93.8 us -> 42.5 us  [per_device(): hidden_grads = lax.psum(hidden_grads, 'ctx')]
    dot_general x56, matrix products: 145 us -> 120 us  [dot(): lax.dot_general(left, right, (dims, ((), ())), preferred_element_type=F32)]
    all_to_all x1, waiting for transfers between devices: 4.69 us -> 20.2 us  [to_rows(): lax.all_to_all(shaped.transpose(1, 0, 2, 3), 'ctx', 0, 0, tiled=True, axi...]
    add x0 -> x3, other arithmetic: none -> 7.82 us  [per_device(): model_grads + lax.ppermute(model_grads, 'ctx', [(dev, dev ^ hop) for dev...]
    unnamed x222 -> x213, local copies, waits for them, and re-layouts: 22.5 us -> 21.3 us
  transfers between devices with their start and end apart: 58 -> 61, of which waited for: 27 -> 29; matrix products, arithmetic and copies ran while one was open for 15% -> 15% of each run, Pallas kernels for 0% -> 0%
where the time goes in v1:
time: 727 us; the launch traced here: 716 us
  waiting for transfers between devices  324 us (45%)
  matrix products  142 us (20%)
  local copies, waits for them, and re-layouts  86.5 us (12%)
  other arithmetic  64.3 us (9%)
  starting transfers between devices  46.5 us (6%)
  blocking collectives  36.8 us (5%)
  between operations  16.3 us (2%)
    dot_general x56, matrix products, dot(): lax.dot_general(left, right, (dims, ((), ())), preferred_element_type=F32)  120 us
    ppermute x3, waiting for transfers between devices, per_device(): lax.ppermute(model_grads, 'ctx', [(dev, dev ^ hop) for dev in range(8)])  113 us
    ppermute x22, waiting for transfers between devices, swap_chip(): return lax.ppermute(values, 'wsh', CHIP_SWAP)  101 us
    psum x1, waiting for transfers between devices, per_device(): hidden_grads = lax.psum(hidden_grads, 'ctx')  42.5 us
    all_to_all x1, waiting for transfers between devices, to_heads(): lax.all_to_all(shaped, 'ctx', 0, 0, tiled=True, axis_index_groups=ctx_gro...  34 us
    ppermute x22, starting transfers between devices, swap_chip(): return lax.ppermute(values, 'wsh', CHIP_SWAP)  28.4 us
    dot_general x6, matrix products, batched(): lax.dot_general(left, right, (((lc,), (rc,)), ((0,), (0,))), preferred_el...  21.8 us
    unnamed x213, local copies, waits for them, and re-layouts  21.3 us
  transfers between devices with their start and end apart: 61, of which 29 were waited for; matrix products, arithmetic and copies ran while one was open for 15% of the time, Pallas kernels for 0%

profile of v1, /device:TPU:0, one launch (start us, length us, event | category | flops | bytes accessed | tf_op | source)
XLA Modules:
  0.0 716.4 jit_solution(11668411908039483659)
XLA Ops:
  20.7 15.3 %collective-permute-done.7 = bf16[7,64,512]{2,1,0:T(8,128)(2,1)} collective-permute-done((bf16[7,64,512]{2,1,0:T(8,128)(2,1)}, bf16[7,64,512]{2,1,0:T(8,128)(2,1)}, u32[]{:S(2)}, u32[]{:S(2)}) %collective-permute-start.7) | collective-permute-done | bytes 458784 | tf_op jit(solution)/shard_map/ppermute | solution.py:41
  72.2 6.4 all-to-all-start
  81.7 34.0 %all-to-all-done = bf16[8,3,128,256]{3,2,1,0:T(8,128)(2,1)} async-done(((bf16[8,3,128,256]{3,2,1,0:T(8,128)(2,1)}), bf16[8,3,128,256]{3,2,1,0:T(8,128)(2,1)}, u32[]{:S(2)}, u32[]{:S(2)}) %all-to-all-start) | async-done | bytes 1572896 | tf_op jit(solution)/shard_map/all_to_all | solution.py:173
  139.2 18.4 %all_to_all.20 = bf16[8,1,128,256]{2,3,1,0:T(8,128)(2,1)} all-to-all(bf16[8,1,128,256]{2,3,1,0:T(8,128)(2,1)S(1)} %copy.165), channel_id=1, replica_groups={{0,4,8,12,16,20,24,28},{1,5,9,13,17,21,25,29},{2,6,10,14,18,22,26,30},{..., dimensions={0} | all-to-all | bytes 1048576 | tf_op jit(solution)/shard_map/all_to_all | solution.py:180
  164.4 11.2 %collective-permute-done.12 = bf16[512,512]{0,1:T(8,128)(2,1)S(1)} collective-permute-done((bf16[512,512]{0,1:T(8,128)(2,1)S(1)}, bf16[512,512]{0,1:T(8,128)(2,1)S(1)}, u32[]{:S(2)}, u32[]{:S(2)}) %collective-permute-start.12) | collective-permute-done | bytes 524320 | tf_op jit(solution)/shard_map/ppermute | solution.py:41
  189.6 11.4 %collective-permute-done.17 = bf16[512,512]{0,1:T(8,128)(2,1)S(1)} collective-permute-done((bf16[512,512]{0,1:T(8,128)(2,1)S(1)}, bf16[512,512]{0,1:T(8,128)(2,1)S(1)}, u32[]{:S(2)}, u32[]{:S(2)}) %collective-permute-start.17) | collective-permute-done | bytes 524320 | tf_op jit(solution)/shard_map/ppermute | solution.py:41
  207.8 11.6 %multiply_add_fusion.1 = f32[512,2048]{0,1:T(8,128)} fusion(f32[512,2048]{0,1:T(8,128)S(1)} %fusion.137, bf16[512,2048]{0,1:T(8,128)(2,1)S(1)} %constant_dynamic-update-slice_fusion.4, bf16[3,2048,2048]{2,1,0:T(8,128)(2,1)} %param.13), kind=kOutput, calls=%fused_computation.37 | convolution fusion | flops 4297064448 | bytes 18874368 | tf_op jit(solution)/shard_map/dot_general | solution.py:21
  219.3 13.1 %multiply_convert_fusion.3 = (bf16[512,2048]{0,1:T(8,128)(2,1)S(1)}, f32[512,2048]{0,1:T(8,128)}) fusion(f32[512,2048]{0,1:T(8,128)} %multiply_add_fusion.1, f32[512,2048]{0,1:T(8,128)S(1)} %fusion.134, bf16[512,2048]{0,1:T(8,128)(2,1)S(1)} %constant_dynamic-update-slice_fusion.4, bf16[3,2048,2048]{2,1,0:T(8,128)(2,1)} %param.13), kind=kOutput, calls=%fused_computation.33 | convolution fusion | flops 4303355904 | bytes 25165824 | tf_op jit(solution)/shard_map/dot_general | solution.py:21
  232.9 7.2 fusion.2
  250.0 10.0 %collective-permute-done.23 = bf16[1,512]{1,0:T(2,128)(2,1)S(1)} collective-permute-done((bf16[1,512]{1,0:T(2,128)(2,1)S(1)}, bf16[1,512]{1,0:T(2,128)(2,1)S(1)}, u32[]{:S(2)}, u32[]{:S(2)}) %collective-permute-start.23) | collective-permute-done | bytes 1056 | tf_op jit(solution)/shard_map/ppermute | solution.py:41
  267.9 12.6 %collective-permute-done.26 = bf16[128,2048]{0,1:T(8,128)(2,1)S(1)} collective-permute-done((bf16[128,2048]{0,1:T(8,128)(2,1)S(1)}, bf16[128,2048]{0,1:T(8,128)(2,1)S(1)}, u32[]{:S(2)}, u32[]{:S(2)}) %collective-permute-start.26) | collective-permute-done | bytes 524320 | tf_op jit(solution)/shard_map/ppermute | solution.py:41
  285.0 10.0 %multiply_convert_fusion.1 = (bf16[512,2048]{0,1:T(8,128)(2,1)S(1)}, bf16[512,2048]{0,1:T(8,128)(2,1)S(1)}) fusion(f32[512,2048]{0,1:T(8,128)} %multiply_add_fusion.1, f32[512,2048]{0,1:T(8,128)} %get-tuple-element.94, f32[512,2048]{0,1:T(8,128)S(1)} %fusion.130, bf16[512,2048]{0,1:T(8,128)(2,1)S(1)} %constant_dynamic-update-slice_fusion, ...), kind=kOutput, calls=%fused_computation.30 | convolution fusion | flops 4309647360 | bytes 27262976 | tf_op jit(solution)/shard_map/dot_general | solution.py:21
  295.4 7.9 %fusion.8 = f32[512,2048]{0,1:T(8,128)S(1)} fusion(bf16[512,2048]{0,1:T(8,128)(2,1)S(1)} %get-tuple-element.37, bf16[3,2048,2048]{2,1,0:T(8,128)(2,1)} %param.13), kind=kOutput, calls=%fused_computation.8 | convolution fusion | flops 4294967296 | bytes 14680064 | tf_op jit(solution)/shard_map/dot_general | solution.py:21
  303.8 6.9 fusion.4
  319.3 12.5 %collective-permute-done.30 = bf16[512,512]{0,1:T(8,128)(2,1)S(1)} collective-permute-done((bf16[512,512]{0,1:T(8,128)(2,1)S(1)}, bf16[512,512]{0,1:T(8,128)(2,1)S(1)}, u32[]{:S(2)}, u32[]{:S(2)}) %collective-permute-start.30) | collective-permute-done | bytes 524320 | tf_op jit(solution)/shard_map/ppermute | solution.py:41
  345.9 12.5 %collective-permute-done.35 = bf16[512,512]{1,0:T(8,128)(2,1)S(1)} collective-permute-done((bf16[512,512]{1,0:T(8,128)(2,1)S(1)}, bf16[512,512]{1,0:T(8,128)(2,1)S(1)}, u32[]{:S(2)}, u32[]{:S(2)}) %collective-permute-start.35) | collective-permute-done | bytes 524320 | tf_op jit(solution)/shard_map/ppermute | solution.py:41
  362.5 18.4 %all_to_all.21 = bf16[8,1,128,256]{3,2,1,0:T(8,128)(2,1)} all-to-all(bf16[8,1,128,256]{3,2,1,0:T(8,128)(2,1)S(1)} %bitcast.546), channel_id=1, replica_groups={{0,4,8,12,16,20,24,28},{1,5,9,13,17,21,25,29},{2,6,10,14,18,22,26,30},{..., dimensions={0} | all-to-all | bytes 1048576 | tf_op jit(solution)/shard_map/all_to_all | solution.py:173
  427.4 20.2 %all-to-all-done.3 = bf16[8,3,128,256]{2,3,1,0:T(8,128)(2,1)} async-done(((bf16[8,3,128,256]{2,3,1,0:T(8,128)(2,1)}), bf16[8,3,128,256]{2,3,1,0:T(8,128)(2,1)}, u32[]{:S(2)}, u32[]{:S(2)}) %all-to-all-start.3) | async-done | bytes 1572896 | tf_op jit(solution)/shard_map/all_to_all | solution.py:180
  517.8 23.2 %collective-permute-done.55 = f32[11,64,512]{2,1,0:T(8,128)S(1)} collective-permute-done((f32[11,64,512]{2,1,0:T(8,128)S(1)}, f32[11,64,512]{2,1,0:T(8,128)S(1)}, u32[]{:S(2)}, u32[]{:S(2)}) %collective-permute-start.55) | collective-permute-done | bytes 1441824 | tf_op jit(solution)/shard_map/ppermute | solution.py:324
  542.4 5.6 add_convert_fusion
  552.9 38.5 %collective-permute-done.56 = f32[11,64,512]{2,1,0:T(8,128)} collective-permute-done((f32[11,64,512]{2,1,0:T(8,128)}, f32[11,64,512]{2,1,0:T(8,128)}, u32[]{:S(2)}, u32[]{:S(2)}) %collective-permute-start.56) | collective-permute-done | bytes 1441824 | tf_op jit(solution)/shard_map/ppermute | solution.py:324
  599.1 8.2 %collective-permute-done.40 = bf16[128,2048]{1,0:T(8,128)(2,1)} collective-permute-done((bf16[128,2048]{1,0:T(8,128)(2,1)S(1)}, bf16[128,2048]{1,0:T(8,128)(2,1)}, u32[]{:S(2)}, u32[]{:S(2)}) %collective-permute-start.40) | collective-permute-done | bytes 524320 | tf_op jit(solution)/shard_map/ppermute | solution.py:41
  609.9 51.1 %collective-permute-done.57 = f32[11,64,512]{2,1,0:T(8,128)} collective-permute-done((f32[11,64,512]{2,1,0:T(8,128)}, f32[11,64,512]{2,1,0:T(8,128)}, u32[]{:S(2)}, u32[]{:S(2)}) %collective-permute-start.57) | collective-permute-done | bytes 1441824 | tf_op jit(solution)/shard_map/ppermute | solution.py:324
  664.2 42.5 %all-reduce.2.cloned.1.call-done = f32[3,64,2048]{2,1,0:T(8,128)} async-done(((f32[3,64,2048]{2,1,0:T(8,128)}), f32[3,64,2048]{2,1,0:T(8,128)}) %all-reduce.2.cloned.1.call-update) | async-done | bytes 1572880 | tf_op jit(solution)/shard_map/psum | solution.py:327
  (544 shorter events, 291.7 us)
Async XLA Ops:
  11.5 27.8 %collective-permute-start = (bf16[128,2048]{0,1:T(8,128)(2,1)S(1)}, bf16[128,2048]{0,1:T(8,128)(2,1)}, u32[]{:S(2)}, u32[]{:S(2)}) collective-permute-start(bf16[128,2048]{0,1:T(8,128)(2,1)S(1)} %bitcast.541), channel_id=1, source_target_pairs={{0,1},{1,0},{2,3},{3,2},{4,5},{5,4},{6,7},{7,6},{8,9},{9,8},{10,11... | collective-permute-start | bytes 1572872 | tf_op jit(solution)/shard_map/ppermute | solution.py:37
  12.1 26.7 %collective-permute-start.1 = (bf16[128,2048]{0,1:T(8,128)(2,1)S(1)}, bf16[128,2048]{0,1:T(8,128)(2,1)}, u32[]{:S(2)}, u32[]{:S(2)}) collective-permute-start(bf16[128,2048]{0,1:T(8,128)(2,1)S(1)} %bitcast.542), channel_id=1, source_target_pairs={{0,2},{2,0},{1,3},{3,1},{4,6},{6,4},{5,7},{7,5},{8,10},{10,8},{9,1... | collective-permute-start | bytes 1572872 | tf_op jit(solution)/shard_map/ppermute | solution.py:41
  14.7 21.3 %collective-permute-start.6 = (bf16[7,64,512]{2,1,0:T(8,128)(2,1)}, bf16[7,64,512]{2,1,0:T(8,128)(2,1)S(1)}, u32[]{:S(2)}, u32[]{:S(2)}) collective-permute-start(bf16[7,64,512]{2,1,0:T(8,128)(2,1)} %get-tuple-element.57), channel_id=1, source_target_pairs={{0,1},{1,0},{2,3},{3,2},{4,5},{5,4},{6,7},{7,6},{8,9},{9,8},{10,11... | collective-permute-start | bytes 1376264 | tf_op jit(solution)/shard_map/ppermute | solution.py:37
  16.0 19.9 %collective-permute-start.7 = (bf16[7,64,512]{2,1,0:T(8,128)(2,1)}, bf16[7,64,512]{2,1,0:T(8,128)(2,1)}, u32[]{:S(2)}, u32[]{:S(2)}) collective-permute-start(bf16[7,64,512]{2,1,0:T(8,128)(2,1)} %get-tuple-element.57), channel_id=1, source_target_pairs={{0,2},{2,0},{1,3},{3,1},{4,6},{6,4},{5,7},{7,5},{8,10},{10,8},{9,1... | collective-permute-start | bytes 1376264 | tf_op jit(solution)/shard_map/ppermute | solution.py:41
  72.2 43.5 %all-to-all-start = ((bf16[8,3,128,256]{3,2,1,0:T(8,128)(2,1)}), bf16[8,3,128,256]{3,2,1,0:T(8,128)(2,1)}, u32[]{:S(2)}, u32[]{:S(2)}) async-start(bf16[8,3,128,256]{3,2,1,0:T(8,128)(2,1)} %bitcast.530), calls=%async_computation | async-start | bytes 3145728 | tf_op jit(solution)/shard_map/all_to_all | solution.py:173
  242.9 19.3 %collective-permute-start.19 = (bf16[128,2048]{0,1:T(8,128)(2,1)}, bf16[128,2048]{0,1:T(8,128)(2,1)}, u32[]{:S(2)}, u32[]{:S(2)}) collective-permute-start(bf16[128,2048]{0,1:T(8,128)(2,1)} %get-tuple-element.44), channel_id=1, source_target_pairs={{0,1},{1,0},{2,3},{3,2},{4,5},{5,4},{6,7},{7,6},{8,9},{9,8},{10,11... | collective-permute-start | bytes 1572872 | tf_op jit(solution)/shard_map/ppermute | solution.py:37
  245.7 16.5 %collective-permute-start.21 = (bf16[128,2048]{0,1:T(8,128)(2,1)}, bf16[128,2048]{0,1:T(8,128)(2,1)}, u32[]{:S(2)}, u32[]{:S(2)}) collective-permute-start(bf16[128,2048]{0,1:T(8,128)(2,1)} %add_convert_fusion.8), channel_id=1, source_target_pairs={{0,2},{2,0},{1,3},{3,1},{4,6},{6,4},{5,7},{7,5},{8,10},{10,8},{9,1... | collective-permute-start | bytes 1572872 | tf_op jit(solution)/shard_map/ppermute | solution.py:41
  247.1 12.9 %collective-permute-start.23 = (bf16[1,512]{1,0:T(2,128)(2,1)S(1)}, bf16[1,512]{1,0:T(2,128)(2,1)S(1)}, u32[]{:S(2)}, u32[]{:S(2)}) collective-permute-start(bf16[1,512]{1,0:T(2,128)(2,1)S(1)} %get-tuple-element.76), channel_id=1, source_target_pairs={{0,2},{2,0},{1,3},{3,1},{4,6},{6,4},{5,7},{7,5},{8,10},{10,8},{9,1... | collective-permute-start | bytes 3080 | tf_op jit(solution)/shard_map/ppermute | solution.py:41
  247.8 13.6 %collective-permute-start.22 = (bf16[1,512]{1,0:T(2,128)(2,1)S(1)}, bf16[1,512]{1,0:T(2,128)(2,1)S(1)}, u32[]{:S(2)}, u32[]{:S(2)}) collective-permute-start(bf16[1,512]{1,0:T(2,128)(2,1)S(1)} %get-tuple-element.76), channel_id=1, source_target_pairs={{0,1},{1,0},{2,3},{3,2},{4,5},{5,4},{6,7},{7,6},{8,9},{9,8},{10,11... | collective-permute-start | bytes 3080 | tf_op jit(solution)/shard_map/ppermute | solution.py:37
  266.1 14.4 %collective-permute-start.26 = (bf16[128,2048]{0,1:T(8,128)(2,1)S(1)}, bf16[128,2048]{0,1:T(8,128)(2,1)S(1)}, u32[]{:S(2)}, u32[]{:S(2)}) collective-permute-start(bf16[128,2048]{0,1:T(8,128)(2,1)S(1)} %get-tuple-element.31), channel_id=1, source_target_pairs={{0,2},{2,0},{1,3},{3,1},{4,6},{6,4},{5,7},{7,5},{8,10},{10,8},{9,1... | collective-permute-start | bytes 1572872 | tf_op jit(solution)/shard_map/ppermute | solution.py:41
  267.6 13.0 %collective-permute-start.25 = (bf16[128,2048]{0,1:T(8,128)(2,1)S(1)}, bf16[128,2048]{0,1:T(8,128)(2,1)S(1)}, u32[]{:S(2)}, u32[]{:S(2)}) collective-permute-start(bf16[128,2048]{0,1:T(8,128)(2,1)S(1)} %get-tuple-element.31), channel_id=1, source_target_pairs={{0,1},{1,0},{2,3},{3,2},{4,5},{5,4},{6,7},{7,6},{8,9},{9,8},{10,11... | collective-permute-start | bytes 1572872 | tf_op jit(solution)/shard_map/ppermute | solution.py:37
  317.7 14.0 %collective-permute-start.30 = (bf16[512,512]{0,1:T(8,128)(2,1)S(1)}, bf16[512,512]{0,1:T(8,128)(2,1)S(1)}, u32[]{:S(2)}, u32[]{:S(2)}) collective-permute-start(bf16[512,512]{0,1:T(8,128)(2,1)S(1)} %add_convert_fusion.6), channel_id=1, source_target_pairs={{0,2},{2,0},{1,3},{3,1},{4,6},{6,4},{5,7},{7,5},{8,10},{10,8},{9,1... | collective-permute-start | bytes 1572872 | tf_op jit(solution)/shard_map/ppermute | solution.py:41
  344.4 14.0 %collective-permute-start.35 = (bf16[512,512]{1,0:T(8,128)(2,1)S(1)}, bf16[512,512]{1,0:T(8,128)(2,1)S(1)}, u32[]{:S(2)}, u32[]{:S(2)}) collective-permute-start(bf16[512,512]{1,0:T(8,128)(2,1)S(1)} %add_convert_fusion.5), channel_id=1, source_target_pairs={{0,2},{2,0},{1,3},{3,1},{4,6},{6,4},{5,7},{7,5},{8,10},{10,8},{9,1... | collective-permute-start | bytes 1572872 | tf_op jit(solution)/shard_map/ppermute | solution.py:41
  407.0 40.6 %all-to-all-start.3 = ((bf16[8,3,128,256]{2,3,1,0:T(8,128)(2,1)}), bf16[8,3,128,256]{2,3,1,0:T(8,128)(2,1)}, u32[]{:S(2)}, u32[]{:S(2)}) async-start(bf16[8,3,128,256]{2,3,1,0:T(8,128)(2,1)} %copy.187), calls=%async_computation.3 | async-start | bytes 3145728 | tf_op jit(solution)/shard_map/all_to_all | solution.py:180
  411.4 295.3 %all-reduce.2.cloned.1.call-start = ((), (), s32[]{:S(2)}) async-start(), calls=%async_computation.4 | async-start | bytes 3145728 | tf_op jit(solution)/shard_map/psum | solution.py:327
  422.6 45.8 %collective-permute-start.52 = (f32[512,16]{0,1:T(8,128)}, f32[512,16]{0,1:T(8,128)}, u32[]{:S(2)}, u32[]{:S(2)}) collective-permute-start(f32[512,16]{0,1:T(8,128)} %add.435), channel_id=1, source_target_pairs={{0,2},{2,0},{1,3},{3,1},{4,6},{6,4},{5,7},{7,5},{8,10},{10,8},{9,1... | collective-permute-start | bytes 98312 | tf_op jit(solution)/shard_map/ppermute | solution.py:41
  424.7 45.1 %collective-permute-start.50 = (f32[512,16]{0,1:T(8,128)}, f32[512,16]{0,1:T(8,128)}, u32[]{:S(2)}, u32[]{:S(2)}) collective-permute-start(f32[512,16]{0,1:T(8,128)} %add.433), channel_id=1, source_target_pairs={{0,2},{2,0},{1,3},{3,1},{4,6},{6,4},{5,7},{7,5},{8,10},{10,8},{9,1... | collective-permute-start | bytes 98312 | tf_op jit(solution)/shard_map/ppermute | solution.py:41
  425.9 52.6 %collective-permute-start.48 = (f32[512,16]{0,1:T(8,128)}, f32[512,16]{0,1:T(8,128)}, u32[]{:S(2)}, u32[]{:S(2)}) collective-permute-start(f32[512,16]{0,1:T(8,128)} %add.431), channel_id=1, source_target_pairs={{0,2},{2,0},{1,3},{3,1},{4,6},{6,4},{5,7},{7,5},{8,10},{10,8},{9,1... | collective-permute-start | bytes 98312 | tf_op jit(solution)/shard_map/ppermute | solution.py:41
  466.8 13.8 %collective-permute-start.36 = (f32[2,512]{1,0:T(2,128)S(1)}, f32[2,512]{1,0:T(2,128)S(1)}, u32[]{:S(2)}, u32[]{:S(2)}) collective-permute-start(f32[2,512]{1,0:T(2,128)S(1)} %pad_maximum_fusion.7), channel_id=1, source_target_pairs={{0,1},{1,0},{2,3},{3,2},{4,5},{5,4},{6,7},{7,6},{8,9},{9,8},{10,11... | collective-permute-start | bytes 12296 | tf_op jit(solution)/shard_map/ppermute | solution.py:37
  508.2 32.8 %collective-permute-start.55 = (f32[11,64,512]{2,1,0:T(8,128)S(1)}, f32[11,64,512]{2,1,0:T(8,128)S(1)}, u32[]{:S(2)}, u32[]{:S(2)}) collective-permute-start(f32[11,64,512]{2,1,0:T(8,128)S(1)} %fusion.84), channel_id=1, source_target_pairs={{0,4},{4,0},{8,12},{12,8},{16,20},{20,16},{24,28},{28,24},{1,5},{5... | collective-permute-start | bytes 4325384 | tf_op jit(solution)/shard_map/ppermute | solution.py:324
  542.4 49.0 %collective-permute-start.56 = (f32[11,64,512]{2,1,0:T(8,128)}, f32[11,64,512]{2,1,0:T(8,128)}, u32[]{:S(2)}, u32[]{:S(2)}) collective-permute-start(f32[11,64,512]{2,1,0:T(8,128)} %add.439), channel_id=1, source_target_pairs={{0,8},{4,12},{8,0},{12,4},{16,24},{20,28},{24,16},{28,20},{1,9},{5... | collective-permute-start | bytes 4325384 | tf_op jit(solution)/shard_map/ppermute | solution.py:324
  550.2 44.4 %collective-permute-start.39 = (bf16[128,2048]{1,0:T(8,128)(2,1)S(1)}, bf16[128,2048]{1,0:T(8,128)(2,1)S(1)}, u32[]{:S(2)}, u32[]{:S(2)}) collective-permute-start(bf16[128,2048]{1,0:T(8,128)(2,1)S(1)} %get-tuple-element.39), channel_id=1, source_target_pairs={{0,1},{1,0},{2,3},{3,2},{4,5},{5,4},{6,7},{7,6},{8,9},{9,8},{10,11... | collective-permute-start | bytes 1572872 | tf_op jit(solution)/shard_map/ppermute | solution.py:37
  552.3 46.8 %collective-permute-start.38 = (bf16[128,2048]{1,0:T(8,128)(2,1)}, bf16[128,2048]{1,0:T(8,128)(2,1)}, u32[]{:S(2)}, u32[]{:S(2)}) collective-permute-start(bf16[128,2048]{1,0:T(8,128)(2,1)} %get-tuple-element.38), channel_id=1, source_target_pairs={{0,1},{1,0},{2,3},{3,2},{4,5},{5,4},{6,7},{7,6},{8,9},{9,8},{10,11... | collective-permute-start | bytes 1572872 | tf_op jit(solution)/shard_map/ppermute | solution.py:37
  594.6 66.4 %collective-permute-start.57 = (f32[11,64,512]{2,1,0:T(8,128)}, f32[11,64,512]{2,1,0:T(8,128)}, u32[]{:S(2)}, u32[]{:S(2)}) collective-permute-start(f32[11,64,512]{2,1,0:T(8,128)} %add.440), channel_id=1, source_target_pairs={{0,16},{4,20},{8,24},{12,28},{16,0},{20,4},{24,8},{28,12},{1,17},{... | collective-permute-start | bytes 4325384 | tf_op jit(solution)/shard_map/ppermute | solution.py:324
  (140 other events, 1232.3 us)
Sparse Core Ops, SparseCore 0:
  552.4 154.2 all-reduce.1
